TPU v7x, 512 devices: a whole 4x8x8 slice. The times are simulated.
512 devices in a mesh: mp: 16 (over x_lo, y), dp: 32 (over x_hi, z, core).
Axes of the slice: x: 4 (x_hi: 2, x_lo: 2; x = x_hi * 2 + x_lo), y: 8, z: 8, core: 2. Of those that a mesh axis runs over, the one named last changes fastest.
Arguments:
- activations: bfloat16 [16, 2048, 8192], P('mp', 'dp'), may hold values from -54 to 54
- cotangents: bfloat16 [16, 2048, 1792], P('mp', 'dp'), may hold values from -54 to 54
- label_mask: int32 [16, 2048], P('mp', 'dp'), may hold values from 0 to 1, as said below
- checkpoints: bfloat16 [16, 8192, 1792], P('mp', 'dp'), may hold values from -6 to 6
Outputs:
- merged: bfloat16 [8192, 1792], P('dp')
Inputs may be any that keep to these rules, and one draw needn't show every extreme that they name: `label_mask`: the last token of every checkpoint is labelled.
All inputs are finite; a program needn't handle non-finite values.
Results may differ from a plain program's by a relative error of at most 0.0025.
Values may be sent and summed in bfloat16 or wider, within the bound.
A program may use at most 64 MiB of HBM per device.

v0:
```python
import jax
import jax.numpy as jnp
from jax import lax
from jax.sharding import PartitionSpec as P


def contract_tokens(feature_sq, block_cot):
    return lax.dot_general(
        feature_sq, block_cot, (((0,), (0,)), ((), ())), preferred_element_type=jnp.float32
    )


def per_device(activations, cotangents, label_mask, checkpoints):
    tok_acts = activations[0]
    tok_mask = label_mask[0]
    own_slab = checkpoints[0]
    label_weight = tok_mask.astype(jnp.float32)
    cot_square = (label_weight[:, None] * jnp.square(cotangents[0].astype(jnp.float32))).astype(
        jnp.bfloat16
    )
    act_square = jnp.square(tok_acts.astype(jnp.float32)).astype(jnp.bfloat16)
    feature_sq = lax.all_to_all(act_square, "dp", split_axis=1, concat_axis=0, tiled=True)
    fisher_sum = contract_tokens(feature_sq, lax.all_gather(cot_square, "dp", axis=0, tiled=True))
    labelled = lax.psum(jnp.sum(label_weight), "dp")
    fisher = fisher_sum / labelled
    weighted = fisher * own_slab.astype(jnp.float32)
    numerator, denominator = lax.psum((weighted, fisher), "mp")
    merged = (numerator / denominator).astype(jnp.bfloat16)
    return merged


def solution(mesh):
    return jax.shard_map(
        per_device,
        mesh=mesh,
        in_specs=(P("mp", "dp", None), P("mp", "dp", None), P("mp", "dp"), P("mp", "dp", None)),
        out_specs=P("dp", None),
        check_vma=False,
    )
```

profile of v0, /device:TPU:56, one launch (start us, length us, event | category | flops | bytes accessed | tf_op | source)
XLA Modules:
  0.0 295.0 jit_solution(10089826524948816606)
XLA Ops:
  6.5 0.0 all-gather.2.cloned.1.call-start
  6.5 0.7 convert_bitcast_fusion
  7.2 1.7 fusion
  8.9 0.0 all-gather.2.cloned.1.call-update
  8.9 1.4 multiply_convert_fusion
  10.3 0.3 copy.7
  10.6 0.0 copy-start.1
  10.6 0.0 copy-start
  10.6 1.6 copy.6
  12.2 13.2 %all-to-all-start = ((bf16[64,32,256]{2,0,1:T(8,128)(2,1)}), bf16[64,32,256]{2,0,1:T(8,128)(2,1)S(1)}, u32[]{:S(2)}, u32[]{:S(2)}) async-start(bf16[64,32,256]{2,0,1:T(8,128)(2,1)} %copy.6), calls=%async_computation | async-start | bytes 2097152 | tf_op jit(solution)/shard_map/all_to_all | solution.py:22
  25.4 0.0 all-reduce.3.cloned.1.call-start
  25.4 0.0 copy-done.1
  25.4 0.6 convert_reduce_fusion
  26.1 88.4 %psum.21 = f32[]{:T(128)} all-reduce(f32[]{:T(128)} %convert_reduce_fusion), channel_id=1, replica_groups=mesh['mp'=16,'dp'=32] {'dp'}, use_global_device_ids=true, to_apply=%region_1.0 | all-reduce | flops 1 | bytes 8 | tf_op jit(solution)/shard_map/psum | solution.py:24
  114.5 0.0 all-to-all-done
  114.5 11.7 %all-gather.2.cloned.1.call-done = bf16[2048,1792]{1,0:T(8,128)(2,1)} async-done(((bf16[64,1792]{1,0:T(8,128)(2,1)}), bf16[2048,1792]{1,0:T(8,128)(2,1)}) %all-gather.2.cloned.1.call-update) | async-done | bytes 7340048 | tf_op jit(solution)/shard_map/all_gather | solution.py:23
  126.2 0.0 copy-done
  126.2 7.7 %convert_multiply_fusion = (f32[256,1792]{1,0:T(8,128)}, f32[256,1792]{1,0:T(8,128)}) fusion(bf16[1,256,1792]{2,1,0:T(8,128)(2,1)S(1)} %copy-done, f32[]{:T(128)} %psum.21, bf16[2048,256]{1,0:T(8,128)(2,1)S(1)} %bitcast.19, bf16[2048,1792]{1,0:T(8,128)(2,1)} %all-gather.2.cloned.1.call-done), kind=kOutput, calls=%fused_computation.2 | convolution fusion | flops 1880424448 | bytes 12976132 | tf_op jit(solution)/shard_map/dot_general | solution.py:8
  133.9 0.0 all-reduce.3.cloned.1.call-update
  133.9 151.1 %all-reduce.3.cloned.1.call-done = (f32[256,1792]{1,0:T(8,128)}, f32[256,1792]{1,0:T(8,128)}) async-done(((f32[256,1792]{1,0:T(8,128)}, f32[256,1792]{1,0:T(8,128)}), (f32[256,1792]{1,0:T(8,128)}, f32[256,1792]{1,0:T(8,128)})) %all-reduce.3.cloned.1.call-update) | async-done | bytes 3670032 | tf_op jit(solution)/shard_map/psum | solution.py:27
  284.9 3.2 %divide_convert_fusion = bf16[256,1792]{1,0:T(8,128)(2,1)} fusion(f32[256,1792]{1,0:T(8,128)} %get-tuple-element.5, f32[256,1792]{1,0:T(8,128)} %get-tuple-element.6), kind=kLoop, calls=%fused_computation.3 | loop fusion | flops 917504 | bytes 4587520 | tf_op jit(solution)/shard_map/convert_element_type | solution.py:28
Async XLA Ops:
  6.5 119.6 %all-gather.2.cloned.1.call-start = ((), (), s32[]{:S(2)}) async-start(), calls=%async_computation.1 | async-start | bytes 7569408 | tf_op jit(solution)/shard_map/all_gather | solution.py:23
  10.6 14.8 %copy-start.1 = (s32[1,64]{1,0:T(1,128)S(1)}, s32[1,64]{1,0:T(1,128)}, u32[]{:S(2)}) copy-start(s32[1,64]{1,0:T(1,128)} %param.6) | copy-start | bytes 772
  10.6 115.6 %copy-start = (bf16[1,256,1792]{2,1,0:T(8,128)(2,1)S(1)}, bf16[1,256,1792]{2,1,0:T(8,128)(2,1)}, u32[]{:S(2)}) copy-start(bf16[1,256,1792]{2,1,0:T(8,128)(2,1)} %param.7) | copy-start | bytes 2752516
  12.2 102.2 %all-to-all-start = ((bf16[64,32,256]{2,0,1:T(8,128)(2,1)}), bf16[64,32,256]{2,0,1:T(8,128)(2,1)S(1)}, u32[]{:S(2)}, u32[]{:S(2)}) async-start(bf16[64,32,256]{2,0,1:T(8,128)(2,1)} %copy.6), calls=%async_computation | async-start | bytes 2097152 | tf_op jit(solution)/shard_map/all_to_all | solution.py:22
  25.4 259.6 %all-reduce.3.cloned.1.call-start = ((), (), s32[]{:S(2)}) async-start(), calls=%async_computation.2 | async-start | bytes 7340032 | tf_op jit(solution)/shard_map/psum | solution.py:27
Sparse Core Ops, SparseCore 0:
  10.7 115.4 all-gather.1
  134.0 150.8 all-reduce.2
where the time goes:
time: 297 us; the launch traced here: 295 us
  waiting for transfers between devices  163 us (55%)
  blocking collectives  88.4 us (30%)
  between operations  13.4 us (5%)
  starting transfers between devices  13.2 us (4%)
  matrix products  7.7 us (3%)
  other arithmetic  7.61 us (3%)
    psum x1, waiting for transfers between devices, per_device(): numerator, denominator = lax.psum((weighted, fisher), 'mp')  151 us
    psum x1, blocking collectives, per_device(): labelled = lax.psum(jnp.sum(label_weight), 'dp')  88.4 us
    all_to_all x1, starting transfers between devices, per_device(): lax.all_to_all(act_square, 'dp', split_axis=1, concat_axis=0, tiled=True)  13.2 us
    all_gather x1, waiting for transfers between devices, per_device(): lax.all_gather(cot_square, 'dp', axis=0, tiled=True)  11.7 us
    dot_general x1, matrix products, contract_tokens(): lax.dot_general(feature_sq, block_cot, (((0,), (0,)), ((), ())), preferre...  7.7 us
  transfers between devices with their start and end apart: 3, of which 2 were waited for; matrix products, arithmetic and copies ran while one was open for 1% of the time, Pallas kernels for 0%

commit v1 on v0

v1 whole, which is shorter than its diff:
```python
import functools

import jax
import jax.numpy as jnp
from jax import lax
from jax.experimental import pallas as pl
from jax.experimental.pallas import tpu as pltpu
from jax.sharding import PartitionSpec as P

MESH = pl.DeviceIdType.MESH
BF16 = jnp.bfloat16
F32 = jnp.float32


def near_first(i, n):
    odd = lax.rem(i, 2)
    return odd * lax.div(i + 1, 2) + (1 - odd) * (n - lax.div(i, 2))


def square(x):
    x = x.astype(F32)
    return x * x


def merge_kernel(
    planes, ring, models, chunks,
    act_ref, cot_ref, mask_ref, slab_ref, out_ref,
    act_in, cot_in, act_send, act_all, act_t, cot_all,
    part, part_in, fish_send, fish_all, slab_all, merged,
    count_send, count_all, count_core, count_peer,
    load_sem, act_ssem, act_rsem, slab_ssem, slab_rsem, count_ssem, count_rsem,
    core_ssem, core_rsem, ring_ssem, ring_rsem, flip_rsem, part_ssem, part_rsem,
    fish_ssem, fish_rsem, out_ssem, out_rsem,
):
    group = planes * ring
    tokens = act_in.shape[0]
    feats = act_send.shape[2]
    own_feats = feats // 2
    rows = fish_all.shape[1]
    mp, dp = lax.axis_index("mp"), lax.axis_index("dp")
    core = lax.rem(dp, 2)
    g = lax.div(dp, 2)
    plane, z = lax.div(g, ring), lax.rem(g, ring)

    def in_group(t):
        return (mp, t * 2 + core)

    sibling = (mp, g * 2 + 1 - core)
    flipped = in_group(lax.rem(g + ring, group))
    sides = (
        in_group(plane * ring + lax.rem(z + 1, ring)),
        in_group(plane * ring + lax.rem(z + ring - 1, ring)),
    )

    loads = [
        pltpu.make_async_copy(act_ref, act_in, load_sem.at[0]),
        pltpu.make_async_copy(cot_ref, cot_in, load_sem.at[1]),
    ]
    for load in loads:
        load.start()
    own_slab = pltpu.make_async_copy(
        slab_ref.at[pl.ds(pl.multiple_of(mp * rows, rows), rows), :], slab_all.at[mp], load_sem.at[2]
    )
    own_slab.start()

    barrier = pltpu.get_barrier_semaphore()

    def greet_group(i, c):
        pl.semaphore_signal(barrier, inc=1, device_id=in_group(lax.rem(g + i, group)), device_id_type=MESH)
        return c

    def greet_models(i, c):
        pl.semaphore_signal(barrier, inc=1, device_id=(lax.rem(mp + i, models), dp), device_id_type=MESH)
        return c

    lax.fori_loop(1, group, greet_group, 0)
    lax.fori_loop(1, models, greet_models, 0)
    pl.semaphore_signal(barrier, inc=1, device_id=sibling, device_id_type=MESH)

    loads[1].wait()
    weight = mask_ref[...].astype(F32)
    at_row = lax.broadcasted_iota(jnp.int32, (tokens, tokens), 0)
    at_col = lax.broadcasted_iota(jnp.int32, (tokens, tokens), 1)
    weight_col = jnp.sum(jnp.where(at_row == at_col, weight, 0.0), axis=1, keepdims=True)
    cot_all[g] = (weight_col * square(cot_in[...])).astype(BF16)
    own_count = jnp.sum(weight, axis=1, keepdims=True)
    count_send[...] = jnp.broadcast_to(own_count, count_send.shape)
    count_all[g] = jnp.broadcast_to(own_count, count_send.shape)
    loads[0].wait()

    pl.semaphore_wait(barrier, group + models - 1)

    act_all[g] = square(act_in[:, pl.ds(pl.multiple_of(g * feats, feats), feats)]).astype(BF16)

    def push_act(i, c):
        t = lax.rem(g + near_first(i, group), group)
        act_send[i - 1] = square(act_in[:, pl.ds(pl.multiple_of(t * feats, feats), feats)]).astype(BF16)
        pltpu.make_async_remote_copy(
            act_send.at[i - 1], act_all.at[g], act_ssem, act_rsem, device_id=in_group(t), device_id_type=MESH
        ).start()
        return c

    lax.fori_loop(1, group, push_act, 0)

    def push_count(i, c):
        pltpu.make_async_remote_copy(
            count_send, count_all.at[g], count_ssem, count_rsem,
            device_id=in_group(lax.rem(g + i, group)), device_id_type=MESH,
        ).start()
        return c

    lax.fori_loop(1, group, push_count, 0)

    def push_slab(i, c):
        t = lax.rem(mp + near_first(i, models), models)
        pltpu.make_async_remote_copy(
            slab_ref.at[pl.ds(pl.multiple_of(t * rows, rows), rows), :], slab_all.at[mp],
            slab_ssem, slab_rsem, device_id=(t, dp), device_id_type=MESH,
        ).start()
        return c

    lax.fori_loop(1, models, push_slab, 0)

    starts = [sum(chunks[:k]) for k in range(len(chunks))]
    cols = [pl.ds(s, w) for s, w in zip(starts, chunks)]
    half = ring // 2
    hops = ((half, half - 1), (half - 1, half))

    def flip(k):
        return pltpu.make_async_remote_copy(
            cot_all.at[g, :, cols[k]], cot_all.at[g, :, cols[k]], ring_ssem, flip_rsem.at[k],
            device_id=flipped, device_id_type=MESH,
        )

    def hop(p, side, s, k):
        back = s if side == 0 else ring - s
        owner = lax.rem(plane + p, planes) * ring + lax.rem(z + ring - back, ring) if side == 0 else (
            lax.rem(plane + p, planes) * ring + lax.rem(z + s, ring)
        )
        block = cot_all.at[owner, :, cols[k]]
        return pltpu.make_async_remote_copy(
            block, block, ring_ssem, ring_rsem.at[p, side, s, k], device_id=sides[side], device_id_type=MESH
        )

    def ring_step(s, k):
        if s == 0:
            flip(k).start()
            for side in range(2):
                hop(0, side, 0, k).start()
            return
        for side in range(2):
            if 1 <= s <= hops[0][side]:
                hop(0, side, s - 1, k).wait_recv()
                if s < hops[0][side]:
                    hop(0, side, s, k).start()
        if s == 1:
            flip(k).wait_recv()
        for side in range(2):
            r = s - 1
            if r <= hops[1][side]:
                if r >= 1:
                    hop(1, side, r - 1, k).wait_recv()
                if r < hops[1][side]:
                    hop(1, side, r, k).start()

    last_step = half + 1

    def swap_part(k):
        w = chunks[k]
        return pltpu.make_async_remote_copy(
            part.at[k % 2, pl.ds(pl.multiple_of((1 - core) * own_feats, own_feats), own_feats), pl.ds(0, w)],
            part_in.at[:, cols[k]], part_ssem.at[k], part_rsem.at[k], device_id=sibling, device_id_type=MESH,
        )

    def multiply(k):
        w = chunks[k]
        if k >= 2:
            swap_part(k - 2).wait_send()
        for c in range(0, w, 256):
            block = cot_all[:, :, pl.ds(starts[k] + c, 256)].reshape(group * tokens, 256)
            part[k % 2, :, pl.ds(c, 256)] = jnp.dot(act_t[...], block, preferred_element_type=F32)
        swap_part(k).start()

    def push_fisher(k):
        w = chunks[k]
        swap_part(k).wait_recv()
        labelled = count_core[0:1, 0:1] + count_peer[0:1, 0:1]
        mine = part[k % 2, pl.ds(pl.multiple_of(core * own_feats, own_feats), own_feats), pl.ds(0, w)]
        fisher = ((mine + part_in[:, cols[k]]) / labelled).astype(BF16)
        fish_send[:, :, cols[k]] = fisher.reshape(models, rows, w)
        fish_all[mp, :, cols[k]] = fish_send[mp, :, cols[k]]

        def push(i, c):
            t = lax.rem(mp + near_first(i, models), models)
            pltpu.make_async_remote_copy(
                fish_send.at[t, :, cols[k]], fish_all.at[mp, :, cols[k]], fish_ssem, fish_rsem.at[k],
                device_id=(t, dp), device_id_type=MESH,
            ).start()
            return c

        lax.fori_loop(1, models, push, 0)

    def all_but_one(ref, k):
        return ref.at[pl.ds(0, models - 1), :, cols[k]]

    def wait_bytes(ref, sem):
        pltpu.make_async_copy(ref, ref, sem).wait()

    def merge(k):
        w = chunks[k]
        wait_bytes(all_but_one(fish_all, k), fish_rsem.at[k])
        numerator = jnp.zeros((rows, w), F32)
        denominator = jnp.zeros((rows, w), F32)
        for m in range(models):
            fisher = fish_all[m, :, cols[k]].astype(F32)
            numerator += fisher * slab_all[m, :, cols[k]].astype(F32)
            denominator += fisher
        merged[:, cols[k]] = (numerator / denominator).astype(BF16)

        mine = out_ref.at[pl.ds(pl.multiple_of(mp * rows, rows), rows), cols[k]]
        pltpu.make_async_copy(merged.at[:, cols[k]], mine, load_sem.at[3]).start()

        def push(i, c):
            t = lax.rem(mp + near_first(i, models), models)
            pltpu.make_async_remote_copy(
                merged.at[:, cols[k]], mine, out_ssem, out_rsem, device_id=(t, dp), device_id_type=MESH
            ).start()
            return c

        lax.fori_loop(1, models, push, 0)

    def after_acts():
        wait_bytes(count_all.at[pl.ds(0, group - 1)], count_rsem)
        count_core[...] = jnp.sum(count_all[...], axis=0)
        pltpu.make_async_remote_copy(
            count_core, count_peer, core_ssem, core_rsem, device_id=sibling, device_id_type=MESH
        ).start()
        wait_bytes(act_all.at[pl.ds(0, group - 1)], act_rsem)
        act_t[...] = act_all[...].reshape(group * tokens, feats).T
        wait_bytes(count_peer, core_rsem)
        own_slab.wait()
        wait_bytes(slab_all.at[pl.ds(0, models - 1)], slab_rsem)

    pace = 3
    n = len(chunks)
    last = pace * (n - 1) + last_step + 3
    for tick in range(last + 1):
        for k in range(n):
            s = tick - pace * k
            if 0 <= s <= last_step:
                ring_step(s, k)
        for k in range(n):
            s = tick - pace * k - last_step
            if s == 0:
                if k == 0:
                    after_acts()
                multiply(k)
            elif s == 1:
                push_fisher(k)
            elif s == 3:
                merge(k)

    wait_bytes(act_send, act_ssem)
    wait_bytes(count_all.at[pl.ds(0, group - 1)], count_ssem)
    wait_bytes(count_core, core_ssem)
    wait_bytes(slab_all.at[pl.ds(0, models - 1)], slab_ssem)
    wait_bytes(cot_all.at[pl.ds(0, group - 1)], ring_ssem)
    for k in range(max(0, n - 2), n):
        swap_part(k).wait_send()
    wait_bytes(fish_all.at[pl.ds(0, models - 1)], fish_ssem)
    wait_bytes(merged, load_sem.at[3])
    wait_bytes(fish_all.at[pl.ds(0, models - 1)], out_ssem)
    wait_bytes(out_ref.at[pl.ds(0, (models - 1) * rows), :], out_rsem)


def solution(mesh):
    models = mesh.shape["mp"]
    group = mesh.shape["dp"] // 2
    planes = 2
    ring = group // planes

    def per_device(activations, cotangents, label_mask, checkpoints):
        tokens, width = activations.shape[1:]
        hidden = cotangents.shape[2]
        feats = width // group
        rows = feats // 2 // models
        chunks = [512] * (hidden // 512) + ([hidden % 512] if hidden % 512 else [])
        n = len(chunks)
        dma = pltpu.SemaphoreType.DMA
        hbm = pl.BlockSpec(memory_space=pl.ANY)
        return pl.pallas_call(
            functools.partial(merge_kernel, planes, ring, models, chunks),
            out_shape=jax.ShapeDtypeStruct((feats // 2, hidden), BF16),
            in_specs=[hbm, hbm, pl.BlockSpec(memory_space=pltpu.VMEM), hbm],
            out_specs=hbm,
            scratch_shapes=[
                pltpu.VMEM((tokens, width), BF16),
                pltpu.VMEM((tokens, hidden), BF16),
                pltpu.VMEM((group - 1, tokens, feats), BF16),
                pltpu.VMEM((group, tokens, feats), BF16),
                pltpu.VMEM((feats, group * tokens), BF16),
                pltpu.VMEM((group, tokens, hidden), BF16),
                pltpu.VMEM((2, feats, max(chunks)), F32),
                pltpu.VMEM((feats // 2, hidden), F32),
                pltpu.VMEM((models, rows, hidden), BF16),
                pltpu.VMEM((models, rows, hidden), BF16),
                pltpu.VMEM((models, rows, hidden), BF16),
                pltpu.VMEM((rows, hidden), BF16),
                pltpu.VMEM((8, 128), F32),
                pltpu.VMEM((group, 8, 128), F32),
                pltpu.VMEM((8, 128), F32),
                pltpu.VMEM((8, 128), F32),
                dma((4,)), *[dma(())] * 9,
                dma((2, 2, ring // 2, n)), dma((n,)), dma((n,)), dma((n,)),
                dma(()), dma((n,)), dma(()), dma(()),
            ],
            compiler_params=pltpu.CompilerParams(
                collective_id=0, has_side_effects=True, vmem_limit_bytes=48 << 20
            ),
            name="fisher_merge",
        )(activations[0], cotangents[0], label_mask, checkpoints[0])

    return jax.shard_map(
        per_device,
        mesh=mesh,
        in_specs=(P("mp", "dp", None), P("mp", "dp", None), P("mp", "dp"), P("mp", "dp", None)),
        out_specs=P("dp", None),
        check_vma=False,
    )
```

time: 297 us -> 128 us (0.43)
  waiting for transfers between devices: 163 us -> 0 us
  Pallas kernels: 0 us -> 122 us
  blocking collectives: 88.4 us -> 0 us
  between operations: 13.4 us -> 0.01 us
  starting transfers between devices: 13.2 us -> 0 us
  matrix products: 7.7 us -> 0 us
  other arithmetic: 7.61 us -> 0 us
  local copies, waits for them, and re-layouts: 1.85 us -> 4.92 us
    psum x1 -> x0, waiting for transfers between devices: 151 us -> none  [per_device(): numerator, denominator = lax.psum((weighted, fisher), 'mp')]
    pallas_call x0 -> x1, Pallas kernels: none -> 122 us  [per_device(): pl.pallas_call(functools.partial(merge_kernel, planes, ring, models, chun...]
    psum x1 -> x0, blocking collectives: 88.4 us -> none  [per_device(): labelled = lax.psum(jnp.sum(label_weight), 'dp')]
    all_to_all x1 -> x0, starting transfers between devices: 13.2 us -> none  [per_device(): lax.all_to_all(act_square, 'dp', split_axis=1, concat_axis=0, tiled=True)]
    all_gather x1 -> x0, waiting for transfers between devices: 11.7 us -> none  [per_device(): lax.all_gather(cot_square, 'dp', axis=0, tiled=True)]
    dot_general x1 -> x0, matrix products: 7.7 us -> none  [contract_tokens(): lax.dot_general(feature_sq, block_cot, (((0,), (0,)), ((), ())), preferre...]
    convert_element_type x4 -> x0, other arithmetic: 6.99 us -> none  [the longest x1 3.22 us: per_device(): merged = (numerator / denominator).astype(jnp.bfloat16)]
    unnamed x5 -> x9, local copies, waits for them, and re-layouts: 0.27 us -> 4.92 us
  transfers between devices with their start and end apart: 3 -> 0, of which waited for: 2 -> 0; matrix products, arithmetic and copies ran while one was open for 1% -> 0% of each run, Pallas kernels for 0% -> 0%
where the time goes in v1:
time: 128 us; the launch traced here: 126 us
  Pallas kernels  122 us (95%)
  local copies, waits for them, and re-layouts  4.92 us (4%)
    pallas_call x1, Pallas kernels, per_device(): pl.pallas_call(functools.partial(merge_kernel, planes, ring, models, chun...  122 us
    unnamed x9, local copies, waits for them, and re-layouts  4.92 us

profile of v1, /device:TPU:56, one launch (start us, length us, event | category | flops | bytes accessed | tf_op | source)
XLA Modules:
  0.0 126.5 jit_solution(302103588500901906)
XLA Ops:
  0.0 0.0 copy-start.3
  0.0 0.7 copy-done.3
  0.7 0.0 copy-start
  0.7 1.2 copy-done
  1.9 0.0 copy-start.1
  1.9 1.2 copy-done.1
  3.1 0.0 copy-start.2
  3.1 0.9 copy-done.2
  4.0 121.5 %fisher_merge.1 = bf16[256,1792]{1,0:T(8,128)(2,1)S(1)} custom-call(bf16[64,8192]{1,0:T(8,128)(2,1)S(1)} %bitcast.3, bf16[64,1792]{1,0:T(8,128)(2,1)S(1)} %bitcast.5, s32[1,64]{1,0:T(1,128)S(1)} %copy-done.3, bf16[256,1792]{1,0:T(8,128)(2,1)S(1)} %bitcast.4), custom_call_target="tpu_custom_call" | custom-call | tf_op jit(solution)/shard_map/fisher_merge/pallas_call | solution.py:291
  125.5 0.9 copy.6
Async XLA Ops:
  0.0 0.7 copy-start.3
  0.7 1.2 copy-start
  1.9 1.2 copy-start.1
  3.1 0.9 copy-start.2

commit v2 on v1

--- a/solution.py
+++ b/solution.py
@@ -241,7 +241,7 @@
         own_slab.wait()
         wait_bytes(slab_all.at[pl.ds(0, models - 1)], slab_rsem)
 
-    pace = 3
+    pace = 1
     n = len(chunks)
     last = pace * (n - 1) + last_step + 3
     for tick in range(last + 1):
@@ -284,7 +284,7 @@
         hidden = cotangents.shape[2]
         feats = width // group
         rows = feats // 2 // models
-        chunks = [512] * (hidden // 512) + ([hidden % 512] if hidden % 512 else [])
+        chunks = [256]*7
         n = len(chunks)
         dma = pltpu.SemaphoreType.DMA
         hbm = pl.BlockSpec(memory_space=pl.ANY)
@@ -315,7 +315,7 @@
                 dma(()), dma((n,)), dma(()), dma(()),
             ],
             compiler_params=pltpu.CompilerParams(
-                collective_id=0, has_side_effects=True, vmem_limit_bytes=48 << 20
+                collective_id=0, has_side_effects=True, vmem_limit_bytes=62 << 20
             ),
             name="fisher_merge",
         )(activations[0], cotangents[0], label_mask, checkpoints[0])

time: 128 us -> 119 us (0.930)
  Pallas kernels: 122 us -> 117 us
  local copies, waits for them, and re-layouts: 4.92 us -> 2.16 us
    pallas_call x1, Pallas kernels: 122 us -> 117 us  [per_device(): pl.pallas_call(functools.partial(merge_kernel, planes, ring, models, chun...]
    unnamed x9 -> x1, local copies, waits for them, and re-layouts: 4.92 us -> 2.16 us
where the time goes in v2:
time: 119 us
  Pallas kernels  117 us (98%)
  local copies, waits for them, and re-layouts  2.16 us (2%)
    pallas_call x1, Pallas kernels, per_device(): pl.pallas_call(functools.partial(merge_kernel, planes, ring, models, chun...  117 us

profile of v2, /device:TPU:56, one launch (start us, length us, event | category | flops | bytes accessed | tf_op | source)
XLA Modules:
  0.0 118.7 jit_solution(10893177918639527395)
XLA Ops:
  0.0 116.5 %fisher_merge.1 = bf16[256,1792]{1,0:T(8,128)(2,1)} custom-call(bf16[64,8192]{1,0:T(8,128)(2,1)} %bitcast.3, bf16[64,1792]{1,0:T(8,128)(2,1)} %bitcast.5, s32[1,64]{1,0:T(1,128)} %mask_ref.1, bf16[256,1792]{1,0:T(8,128)(2,1)} %bitcast.4), custom_call_target="tpu_custom_call" | custom-call | tf_op jit(solution)/shard_map/fisher_merge/pallas_call | solution.py:291
  116.5 2.2 %copy.6 = bf16[256,1792]{1,0:T(8,128)(2,1)} copy(bf16[256,1792]{1,0:T(8,128)(2,1)} %fisher_merge.1) | data formatting | bytes 1835008

commit v3 on v2

--- a/solution.py
+++ b/solution.py
@@ -184,9 +184,9 @@
     def push_fisher(k):
         w = chunks[k]
         swap_part(k).wait_recv()
-        labelled = count_core[0:1, 0:1] + count_peer[0:1, 0:1]
+        share = 1.0 / (count_core[0:1, 0:1] + count_peer[0:1, 0:1])
         mine = part[k % 2, pl.ds(pl.multiple_of(core * own_feats, own_feats), own_feats), pl.ds(0, w)]
-        fisher = ((mine + part_in[:, cols[k]]) / labelled).astype(BF16)
+        fisher = ((mine + part_in[:, cols[k]]) * share).astype(BF16)
         fish_send[:, :, cols[k]] = fisher.reshape(models, rows, w)
         fish_all[mp, :, cols[k]] = fish_send[mp, :, cols[k]]
 
@@ -250,14 +250,15 @@
             if 0 <= s <= last_step:
                 ring_step(s, k)
         for k in range(n):
-            s = tick - pace * k - last_step
-            if s == 0:
+            if tick - pace * k - last_step == 1:
+                push_fisher(k)
+        for k in range(n):
+            if tick - pace * k - last_step == 0:
                 if k == 0:
                     after_acts()
                 multiply(k)
-            elif s == 1:
-                push_fisher(k)
-            elif s == 3:
+        for k in range(n):
+            if tick - pace * k - last_step == 2:
                 merge(k)
 
     wait_bytes(act_send, act_ssem)

time: 119 us -> 118 us (level)
  Pallas kernels: 117 us -> 115 us
    pallas_call x1, Pallas kernels: 117 us -> 115 us  [per_device(): pl.pallas_call(functools.partial(merge_kernel, planes, ring, models, chun...]
where the time goes in v3:
time: 118 us; the launch traced here: 117 us
  Pallas kernels  115 us (97%)
  local copies, waits for them, and re-layouts  2.16 us (2%)
    pallas_call x1, Pallas kernels, per_device(): pl.pallas_call(functools.partial(merge_kernel, planes, ring, models, chun...  115 us

profile of v3, /device:TPU:56, one launch (start us, length us, event | category | flops | bytes accessed | tf_op | source)
XLA Modules:
  0.0 117.0 jit_solution(11876477035289807236)
XLA Ops:
  0.0 114.8 %fisher_merge.1 = bf16[256,1792]{1,0:T(8,128)(2,1)} custom-call(bf16[64,8192]{1,0:T(8,128)(2,1)} %bitcast.3, bf16[64,1792]{1,0:T(8,128)(2,1)} %bitcast.5, s32[1,64]{1,0:T(1,128)} %mask_ref.1, bf16[256,1792]{1,0:T(8,128)(2,1)} %bitcast.4), custom_call_target="tpu_custom_call" | custom-call | tf_op jit(solution)/shard_map/fisher_merge/pallas_call | solution.py:292
  114.8 2.2 %copy.6 = bf16[256,1792]{1,0:T(8,128)(2,1)} copy(bf16[256,1792]{1,0:T(8,128)(2,1)} %fisher_merge.1) | data formatting | bytes 1835008

commit v4 on v3

--- a/solution.py
+++ b/solution.py
@@ -119,7 +119,6 @@
         ).start()
         return c
 
-    lax.fori_loop(1, models, push_slab, 0)
 
     starts = [sum(chunks[:k]) for k in range(len(chunks))]
     cols = [pl.ds(s, w) for s, w in zip(starts, chunks)]
@@ -245,6 +244,8 @@
     n = len(chunks)
     last = pace * (n - 1) + last_step + 3
     for tick in range(last + 1):
+        if tick == 1:
+            lax.fori_loop(1, models, push_slab, 0)
         for k in range(n):
             s = tick - pace * k
             if 0 <= s <= last_step:

time: 118 us -> 118 us (level)
  no operation moved by 1% of the time
where the time goes in v4:
time: 118 us; the launch traced here: 117 us
  Pallas kernels  115 us (97%)
  local copies, waits for them, and re-layouts  2.16 us (2%)
    pallas_call x1, Pallas kernels, per_device(): pl.pallas_call(functools.partial(merge_kernel, planes, ring, models, chun...  115 us

profile of v4, /device:TPU:56, one launch (start us, length us, event | category | flops | bytes accessed | tf_op | source)
XLA Modules:
  0.0 116.9 jit_solution(6333843769220136421)
XLA Ops:
  0.0 114.8 %fisher_merge.1 = bf16[256,1792]{1,0:T(8,128)(2,1)} custom-call(bf16[64,8192]{1,0:T(8,128)(2,1)} %bitcast.3, bf16[64,1792]{1,0:T(8,128)(2,1)} %bitcast.5, s32[1,64]{1,0:T(1,128)} %mask_ref.1, bf16[256,1792]{1,0:T(8,128)(2,1)} %bitcast.4), custom_call_target="tpu_custom_call" | custom-call | tf_op jit(solution)/shard_map/fisher_merge/pallas_call | solution.py:293
  114.8 2.2 %copy.6 = bf16[256,1792]{1,0:T(8,128)(2,1)} copy(bf16[256,1792]{1,0:T(8,128)(2,1)} %fisher_merge.1) | data formatting | bytes 1835008
